TPU v7x, 32 devices: a whole 2x2x4 slice. The times are simulated.
32 devices in a mesh: st: 8 (over y, x, core), fq: 4 (over z).
Axes of the slice: x: 2, y: 2, z: 4, core: 2. Of those that a mesh axis runs over, the one named last changes fastest.
Arguments:
- signals: bfloat16 [512, 16384], P(('st', 'fq')), may hold values from -6 to 6
- freq_bins: int32 [1024], replicated, may hold values from 1 to 8191, as said below
- sensor_station: int32 [512], P('st'), may hold values from 0 to 255, as said below
- gain: bfloat16 [512, 768], P('st'), may hold values from -1.5 to 1.5
- damping: float32 [256, 768], P('st'), may hold values from 0 to 1
- damping_up: float32 [256, 768], P('st'), may hold values from 0 to 1
- phase_speed: float32 [768], replicated, may hold values from 0.5 to 4
Outputs:
- estimate: bfloat16 [256, 768, 1024], P(('st', 'fq'))
Inputs may be any that keep to these rules, and one draw needn't show every extreme that they name: `freq_bins`: distinct bin numbers. `sensor_station`: sensor s sits at one of the 32 stations starting at (s // 64) * 32.
All inputs are finite; a program needn't handle non-finite values.
Results may differ from a plain program's by a relative error of at most 0.015.
Values may be sent and summed in bfloat16 or wider, within the bound.
A program may use at most 320 MiB of HBM per device.

v0:
```python
import math
import jax
import jax.numpy as jnp
from jax import lax
from jax.sharding import PartitionSpec as P

NT = 16384
NF = 1024
TOUT = 1024


def shifted(block, axis, distance):
    devices = range(lax.axis_size(axis))
    route = [(i - distance, i) for i in devices if i - distance in devices]
    return lax.ppermute(block, axis, route)


def cmul(left, right):
    return jnp.stack(
        [left[0] * right[0] - left[1] * right[1], left[0] * right[1] + left[1] * right[0]]
    )


def phases(steps, freq_bins):
    angle = (steps[:, None] * freq_bins[None, :] % NT).astype(jnp.float32) * (2 * math.pi / NT)
    return (jnp.cos(angle), jnp.sin(angle))


def base_table(count, freq_bins):
    fine = min(count, 128)
    coarse = count // fine
    fine_cos, fine_sin = phases(lax.iota(jnp.int32, fine), freq_bins)
    big_cos, big_sin = phases(lax.iota(jnp.int32, coarse) * fine, freq_bins)
    table_cos = big_cos[:, None, :] * fine_cos[None] - big_sin[:, None, :] * fine_sin[None]
    table_sin = big_sin[:, None, :] * fine_cos[None] + big_cos[:, None, :] * fine_sin[None]
    return (table_cos.reshape(count, -1), table_sin.reshape(count, -1))


def phase_rotated(base_cos, base_sine_table, offset, freq_bins):
    row_cos, row_sin = phases(jnp.reshape(offset, (1,)).astype(jnp.int32), freq_bins)
    return (
        base_cos * row_cos - base_sine_table * row_sin,
        base_sine_table * row_cos + base_cos * row_sin,
    )


def on_device(signals, freq_bins, sensor_station, gain, damping, damping_up, phase_speed):
    sens_dev = signals.shape[0]
    width = min(NT, 2048)
    base_cos, base_sine_table = base_table(width, freq_bins)

    def add_block(index, total):
        start = index * width
        times = start + lax.iota(jnp.int32, width)
        hann = 0.5 - 0.5 * jnp.cos(times.astype(jnp.float32) * (2 * math.pi / NT))
        piece = lax.dynamic_slice_in_dim(signals, start, width, 1)
        windowed = (piece.astype(jnp.float32) * hann[None, :]).astype(jnp.bfloat16)
        turned_cos, shifted_imaginary_factor = phase_rotated(
            base_cos, base_sine_table, start, freq_bins
        )
        table = jnp.concatenate(
            [
                (turned_cos / math.sqrt(NT)).astype(jnp.bfloat16),
                (shifted_imaginary_factor / math.sqrt(NT)).astype(jnp.bfloat16),
            ],
            axis=1,
        )
        return total + jnp.dot(windowed, table, preferred_element_type=jnp.float32)

    spectra = lax.fori_loop(0, NT // width, add_block, jnp.zeros((sens_dev, 2 * NF), jnp.float32))
    spec_re = spectra[:, :NF].astype(jnp.bfloat16)
    spec_im = (-spectra[:, NF:]).astype(jnp.bfloat16)
    spec_re, spec_im = (
        lax.all_to_all(spec_re, "fq", split_axis=1, concat_axis=0, tiled=True),
        lax.all_to_all(spec_im, "fq", split_axis=1, concat_axis=0, tiled=True),
    )
    sens_block = spec_re.shape[0]
    freq_dev = spec_re.shape[1]
    width_state = gain.shape[1]
    st_dev = damping.shape[0]
    own_bins = lax.dynamic_slice_in_dim(freq_bins, lax.axis_index("fq") * freq_dev, freq_dev)
    theta = 2 * math.pi * (own_bins.astype(jnp.float32) / NT)[:, None] * phase_speed[None, :]
    rot_down = jnp.stack([jnp.cos(theta), -jnp.sin(theta)])
    rot_up = jnp.stack([jnp.cos(theta), jnp.sin(theta)])
    local = sensor_station - lax.axis_index("st") * st_dev
    onehot = (local[None, :] == lax.iota(jnp.int32, st_dev)[:, None]).astype(jnp.bfloat16)
    spec_own = jnp.stack([spec_re, spec_im]).transpose(0, 2, 1)
    selected = onehot[:, None, None, :] * spec_own[None]
    forcing = jnp.dot(selected.reshape(-1, sens_block), gain, preferred_element_type=jnp.float32)
    forcing = forcing.reshape(st_dev, 2, freq_dev, width_state)
    zeros = jnp.zeros((2, freq_dev, width_state), jnp.float32)
    identity = jnp.stack(
        [
            jnp.ones((freq_dev, width_state), jnp.float32),
            jnp.zeros((freq_dev, width_state), jnp.float32),
        ]
    )

    def march_down(carry, inputs):
        state, product = carry
        term, rate = inputs
        factor = rate[None, None, :] * rot_down
        state = cmul(factor, state) + term
        return ((state, cmul(factor, product)), state)

    (last_down, block_down), downstream_fields = lax.scan(
        march_down, (zeros, identity), (forcing, damping)
    )

    def march_upward(carry, inputs):
        state, product = carry
        term, rate, lower = inputs
        factor = rate[None, None, :] * rot_up
        state = cmul(factor, state) + term
        return ((state, cmul(factor, product)), state + lower)

    (first_up, block_up), partial_sum = lax.scan(
        march_upward, (zeros, identity), (forcing, damping_up, downstream_fields), reverse=True
    )

    def relay(turn, carry):
        from_below, from_above = carry
        output_downward = cmul(block_down, from_below) + last_down
        out_up = cmul(block_up, from_above) + first_up
        from_below = shifted(output_downward.astype(jnp.bfloat16), "st", 1).astype(
            output_downward.dtype
        )
        from_above = shifted(out_up.astype(jnp.bfloat16), "st", -1).astype(out_up.dtype)
        return (from_below, from_above)

    from_below, from_above = lax.fori_loop(0, lax.axis_size("st") - 1, relay, (zeros, zeros))

    def carry_down(state, rate):
        state = cmul(rate[None, None, :] * rot_down, state)
        return (state, state)

    ending_down, lifted_down = lax.scan(carry_down, from_below, damping)

    def carry_up(state, inputs):
        rate, base, lower = inputs
        state = cmul(rate[None, None, :] * rot_up, state)
        return (state, (base + lower + state).astype(jnp.bfloat16))

    ending_up, state_all = lax.scan(
        carry_up, from_above, (damping_up, partial_sum, lifted_down), reverse=True
    )
    out_cos, out_sin = base_table(TOUT, freq_bins)
    out_cos, out_sin = phase_rotated(out_cos, out_sin, NT - TOUT, freq_bins)
    inverse = jnp.stack(
        [
            (out_cos.T / math.sqrt(NF)).astype(jnp.bfloat16),
            (-out_sin.T / math.sqrt(NF)).astype(jnp.bfloat16),
        ]
    )
    return jnp.einsum(
        "kcfm,cft->kmt",
        lax.all_to_all(state_all, "fq", split_axis=0, concat_axis=2, tiled=True),
        inverse,
        preferred_element_type=jnp.float32,
    ).astype(jnp.bfloat16)


def solution(mesh):
    placed = (P(("st", "fq"), None), P(), P("st"), P("st", None), P("st", None), P("st", None), P())
    return jax.shard_map(
        on_device,
        mesh=mesh,
        in_specs=placed,
        out_specs=P(("st", "fq"), None, None),
        check_vma=False,
    )
```

profile of v0, /device:TPU:4, one launch (start us, length us, event | category | flops | bytes accessed | tf_op | source)
XLA Modules:
  0.0 2022.5 jit_solution(1297842721965463363)
XLA Ops:
  3.8 110.0 %while.98 = (s32[]{:T(128)}, f32[16,2048]{1,0:T(8,128)S(1)}, bf16[16,16384]{1,0:T(8,128)(2,1)}, s32[1024]{0:T(1024)}, f32[128,1024]{1,0:T(8,128)S(1)}, /*index=5...) while((s32[]{:T(128)}, f32[16,2048]{1,0:T(8,128)S(1)}, ...), condition=%wide.region_1.2_spmd.clone.clone.clone, body=%wide.region_0.1_spmd.clone.clone.clone.sunk | while | flops 184737792 | bytes 51876020 | solution.py:70
  7.0 5.8 fusion.92
  12.9 4.7 fusion.93
  20.7 5.8 fusion.92
  26.6 4.7 fusion.93
  34.5 5.8 fusion.92
  40.4 4.7 fusion.93
  48.2 5.8 fusion.92
  54.1 4.7 fusion.93
  62.0 5.8 fusion.92
  67.9 4.7 fusion.93
  75.7 5.8 fusion.92
  81.6 4.7 fusion.93
  89.5 5.8 fusion.92
  95.3 4.7 fusion.93
  103.2 5.8 fusion.92
  109.1 4.7 fusion.93
  114.5 4.9 all-to-all-start
  120.1 4.0 multiply_sine_fusion
  125.0 4.8 all-to-all-start.1
  131.7 3.7 all-to-all-done.1
  135.5 20.2 fusion.44
  155.7 16.3 broadcast.585.clone
  173.3 316.1 %while.95 = (s32[]{:T(128)}, f32[2,256,768]{2,1,0:T(8,128)}, f32[2,256,768]{2,1,0:T(8,128)}, f32[32,2,256,768]{3,2,1,0:T(8,128)}, f32[32,768]{1,0:T(8,128)}, /*i...) while((s32[]{:T(128)}, f32[2,256,768]{2,1,0:T(8,128)}, ...), condition=%wide.region_3.4_spmd.clone, body=%wide.region_2.3_spmd.clone.sunk | while | flops 5111811 | bytes 33040012 | solution.py:106
  489.4 16.2 broadcast.585.clone.1
  507.0 333.9 %while.96 = (s32[]{:T(128)}, f32[2,256,768]{2,1,0:T(8,128)}, f32[2,256,768]{2,1,0:T(8,128)}, f32[32,2,256,768]{3,2,1,0:T(8,128)}, f32[32,768]{1,0:T(8,128)}, /*i...) while((s32[]{:T(128)}, f32[2,256,768]{2,1,0:T(8,128)}, ...), condition=%wide.region_5.6_spmd.clone, body=%wide.region_4.5_spmd.clone.sunk | while | flops 5505028 | bytes 34612392 | solution.py:117
  530.5 3.4 fusion.87
  540.9 3.4 fusion.87
  551.4 3.4 fusion.87
  561.8 3.4 fusion.87
  572.4 3.4 fusion.87
  582.8 3.4 fusion.87
  635.0 3.4 fusion.87
  645.5 3.4 fusion.87
  666.4 3.4 fusion.87
  676.9 3.4 fusion.87
  749.9 3.4 fusion.87
  770.9 3.4 fusion.87
  781.3 3.4 fusion.87
  791.8 3.4 fusion.87
  802.3 3.4 fusion.87
  841.0 217.8 %while.97 = (s32[]{:T(128)}, f32[2,256,768]{2,1,0:T(8,128)}, f32[2,256,768]{2,1,0:T(8,128)}, f32[2,256,768]{2,1,0:T(8,128)}, f32[2,256,768]{2,1,0:T(8,128)}, /*i...) while((s32[]{:T(128)}, f32[2,256,768]{2,1,0:T(8,128)}, ...), condition=%wide.region_7.8_spmd.clone, body=%wide.region_6.7_spmd.clone.sunk | while | flops 6291459 | bytes 66060612 | solution.py:131
  852.1 10.8 collective-permute-done.1
  865.4 3.4 collective-permute-done
  882.8 11.7 collective-permute-done.1
  906.5 3.7 collective-permute-start.1
  913.2 12.5 collective-permute-done.1
  936.8 4.7 collective-permute-start.1
  944.5 12.8 collective-permute-done.1
  968.4 4.7 collective-permute-start.1
  976.1 13.1 collective-permute-done.1
  1000.3 4.7 collective-permute-start.1
  1008.0 13.5 collective-permute-done.1
  1032.5 4.7 collective-permute-start.1
  1040.2 13.8 collective-permute-done.1
  1058.8 16.2 broadcast.585
  1075.0 137.9 %while.93 = (s32[]{:T(128)}, f32[2,256,768]{2,1,0:T(8,128)}, f32[32,2,256,768]{3,2,1,0:T(8,128)}, f32[32,768]{1,0:T(8,128)}, f32[2,256,768]{2,1,0:T(8,128)S(1)}, /*index=5*/s32[]{:T(128)}) while((s32[]{:T(128)}, f32[2,256,768]{2,1,0:T(8,128)}, f32[32,2,256,768]{3,2,1,0:T(8,128)}, f32[32,768]{1,0:T(8,128)}, f32[2,256,768]{2,1,0:T(8,128)S(1)}, ...), condition=%wide.region_9.10_spmd, body=%wide.region_8.9_spmd.sunk | while | flops 1966082 | bytes 18884196 | solution.py:137
  1212.9 8.8 broadcast_in_dim.20
  1221.7 138.6 %while.94 = (s32[]{:T(128)}, f32[2,256,768]{2,1,0:T(8,128)S(1)}, bf16[32,2,256,768]{3,2,1,0:T(8,128)(2,1)}, f32[32,768]{1,0:T(8,128)}, f32[2,256,768]{2,1,0:T(8,...) while((s32[]{:T(128)}, f32[2,256,768]{2,1,0:T(8,128)S(1)}, ...), condition=%wide.region_11.12_spmd, body=%wide.region_10.11_spmd.sunk | while | flops 3538947 | bytes 16524401 | solution.py:144
  1360.3 8.8 all-to-all-start.2
  1375.8 535.3 %all-to-all-done.2 = bf16[32,2,256,768]{3,2,1,0:T(8,128)(2,1)} async-done(((bf16[32,2,256,768]{3,2,1,0:T(8,128)(2,1)}), bf16[32,2,256,768]{3,2,1,0:T(8,128)(2,1)}, u32[]{:S(2)}, u32[]{:S(2)}) %all-to-all-start.2) | async-done | bytes 25165856 | tf_op jit(solution)/shard_map/all_to_all | solution.py:157
  1911.1 38.9 %copy.26 = bf16[4,8,2,256,768]{3,0,4,2,1:T(4,128)(2,1)} copy(bf16[4,8,2,256,768]{4,3,2,1,0:T(8,128)(2,1)} %bitcast.10) | data formatting | bytes 50331648 | tf_op jit(solution)/shard_map/all_to_all | solution.py:157
  1949.9 40.6 %all_to_all.46 = bf16[8,2,1024,768]{2,3,1,0:T(8,128)(2,1)} reshape(bf16[8,2,4,256,768]{3,2,4,1,0:T(4,128)(2,1)} %bitcast.140) | data formatting | bytes 50331648 | tf_op jit(solution)/shard_map/all_to_all | solution.py:157
  1990.5 32.0 %bitcast_convert_fusion = bf16[8,768,1024]{2,1,0:T(8,128)(2,1)} fusion(bf16[8,2,1024,768]{2,3,1,0:T(8,128)(2,1)} %all_to_all.46, bf16[1,1024,1024]{2,1,0:T(8,128)(2,1)} %get-tuple-element.875, bf16[1,1024,1024]{2,1,0:T(8,128)(2,1)S(1)} %get-tuple-element.874), kind=kOutput, calls=%fused_computation.80 | convolution fusion | flops 25778192384 | bytes 41943040 | tf_op jit(solution)/shard_map/kcfm,cft->kmt/dot_general | solution.py:155
  (1058 shorter events, 1018.3 us)
Async XLA Ops:
  0.0 135.5 %copy-start = (bf16[64,768]{1,0:T(8,128)(2,1)S(1)}, bf16[64,768]{1,0:T(8,128)(2,1)}, u32[]{:S(2)}) copy-start(bf16[64,768]{1,0:T(8,128)(2,1)} %param.22) | copy-start | bytes 294916
  3.8 116.3 %copy-start.16 = (f32[768]{0:T(1024)S(1)}, f32[768]{0:T(1024)}, u32[]{:S(2)}) copy-start(f32[768]{0:T(1024)} %param.25) | copy-start | bytes 9220
  113.8 16.0 copy-start.11
  113.8 16.0 copy-start.13
  113.8 10.3 copy-start.18
  114.5 10.5 all-to-all-start
  125.0 10.5 all-to-all-start.1
  155.7 16.3 copy-start.17
  183.5 1.9 copy-start.4
  193.4 1.9 copy-start.4
  203.3 1.9 copy-start.4
  213.1 1.9 copy-start.4
  223.0 1.9 copy-start.4
  232.9 1.9 copy-start.4
  242.7 1.9 copy-start.4
  252.6 1.9 copy-start.4
  262.5 1.9 copy-start.4
  272.4 1.9 copy-start.4
  282.2 1.9 copy-start.4
  292.2 1.9 copy-start.4
  302.1 1.9 copy-start.4
  312.0 1.9 copy-start.4
  321.8 1.9 copy-start.4
  331.8 1.9 copy-start.4
  351.5 1.9 copy-start.4
  361.5 1.9 copy-start.4
  371.4 1.9 copy-start.4
  381.3 1.9 copy-start.4
  391.2 1.9 copy-start.4
  401.1 1.9 copy-start.4
  410.9 1.9 copy-start.4
  420.8 1.9 copy-start.4
  430.7 1.9 copy-start.4
  440.7 1.9 copy-start.4
  450.5 1.9 copy-start.4
  460.5 1.9 copy-start.4
  470.4 1.9 copy-start.4
  480.3 1.9 copy-start.4
  845.7 3.0 copy-start.10
  846.7 16.2 collective-permute-start.1
  849.7 19.0 collective-permute-start
  876.3 3.0 copy-start.10
  877.3 17.1 collective-permute-start.1
  880.4 17.5 collective-permute-start
  905.5 4.8 copy-start.10
  906.5 19.2 collective-permute-start.1
  911.3 16.9 collective-permute-start
  935.7 5.8 copy-start.10
  936.8 20.6 %collective-permute-start.1 = (bf16[2,256,768]{2,1,0:T(8,128)(2,1)}, bf16[2,256,768]{2,1,0:T(8,128)(2,1)}, u32[]{:S(2)}, u32[]{:S(2)}) collective-permute-start(bf16[2,256,768]{2,1,0:T(8,128)(2,1)} %fusion.89), channel_id=1, source_target_pairs={{4,0},{8,4},{12,8},{16,12},{20,16},{24,20},{28,24},{5,1},{9,5},{13... | collective-permute-start | bytes 2359304 | tf_op jit(solution)/shard_map/while/body/eval_jaxpr/ppermute | solution.py:15
  942.6 17.2 collective-permute-start
  967.3 5.8 copy-start.10
  968.4 20.9 %collective-permute-start.1 = (bf16[2,256,768]{2,1,0:T(8,128)(2,1)}, bf16[2,256,768]{2,1,0:T(8,128)(2,1)}, u32[]{:S(2)}, u32[]{:S(2)}) collective-permute-start(bf16[2,256,768]{2,1,0:T(8,128)(2,1)} %fusion.89), channel_id=1, source_target_pairs={{4,0},{8,4},{12,8},{16,12},{20,16},{24,20},{28,24},{5,1},{9,5},{13... | collective-permute-start | bytes 2359304 | tf_op jit(solution)/shard_map/while/body/eval_jaxpr/ppermute | solution.py:15
  974.2 17.5 collective-permute-start
  999.2 5.8 copy-start.10
  1000.3 21.2 %collective-permute-start.1 = (bf16[2,256,768]{2,1,0:T(8,128)(2,1)}, bf16[2,256,768]{2,1,0:T(8,128)(2,1)}, u32[]{:S(2)}, u32[]{:S(2)}) collective-permute-start(bf16[2,256,768]{2,1,0:T(8,128)(2,1)} %fusion.89), channel_id=1, source_target_pairs={{4,0},{8,4},{12,8},{16,12},{20,16},{24,20},{28,24},{5,1},{9,5},{13... | collective-permute-start | bytes 2359304 | tf_op jit(solution)/shard_map/while/body/eval_jaxpr/ppermute | solution.py:15
  1006.1 17.8 collective-permute-start
  1031.4 5.8 copy-start.10
  1032.5 21.5 %collective-permute-start.1 = (bf16[2,256,768]{2,1,0:T(8,128)(2,1)}, bf16[2,256,768]{2,1,0:T(8,128)(2,1)}, u32[]{:S(2)}, u32[]{:S(2)}) collective-permute-start(bf16[2,256,768]{2,1,0:T(8,128)(2,1)} %fusion.89), channel_id=1, source_target_pairs={{4,0},{8,4},{12,8},{16,12},{20,16},{24,20},{28,24},{5,1},{9,5},{13... | collective-permute-start | bytes 2359304 | tf_op jit(solution)/shard_map/while/body/eval_jaxpr/ppermute | solution.py:15
  1038.3 18.1 collective-permute-start
  1212.9 8.8 copy-start.8
  1360.3 8.8 copy-start.14
  1360.3 9.0 copy-start.12
  1360.3 550.7 %all-to-all-start.2 = ((bf16[32,2,256,768]{3,2,1,0:T(8,128)(2,1)}), bf16[32,2,256,768]{3,2,1,0:T(8,128)(2,1)}, u32[]{:S(2)}, u32[]{:S(2)}) async-start(bf16[32,2,256,768]{3,2,1,0:T(8,128)(2,1)} %get-tuple-element.577), calls=%async_computation.2 | async-start | bytes 50331648 | tf_op jit(solution)/shard_map/all_to_all | solution.py:157
  1990.5 32.0 %copy-start.1 = (bf16[64,768]{1,0:T(8,128)(2,1)S(1)}, bf16[64,768]{1,0:T(8,128)(2,1)}, u32[]{:S(2)}) copy-start(bf16[64,768]{1,0:T(8,128)(2,1)} %param.22) | copy-start | bytes 294916
  (95 other events, 154.4 us)
where the time goes:
time: 2040 us; the launch traced here: 2020 us
  other arithmetic  925 us (45%)
  waiting for transfers between devices  632 us (31%)
  local copies, waits for them, and re-layouts  312 us (15%)
  matrix products  89.8 us (4%)
  starting transfers between devices  59.2 us (3%)
    all_to_all x1, waiting for transfers between devices, on_device(): lax.all_to_all(state_all, 'fq', split_axis=0, concat_axis=2, tiled=True)  535 us
    dynamic_update_slice x96, other arithmetic, on_device(): lax.scan(march_down, (zeros, identity), (forcing, damping))  259 us
    while x78, other arithmetic  119 us
    dynamic_update_slice x32, other arithmetic, on_device(): lax.scan(carry_up, from_above, (damping_up, partial_sum, lifted_down), re...  100 us
    dynamic_slice x128, local copies, waits for them, and re-layouts, on_device(): lax.scan(march_down, (zeros, identity), (forcing, damping))  96.4 us
    ppermute x14, waiting for transfers between devices, shifted(): return lax.ppermute(block, axis, route)  92.6 us
    add x32, other arithmetic, march_upward(): state = cmul(factor, state) + term  89.2 us
    add x32, other arithmetic, march_down(): state = cmul(factor, state) + term  88.3 us
  transfers between devices with their start and end apart: 17, of which 12 were waited for; matrix products, arithmetic and copies ran while one was open for 2% of the time, Pallas kernels for 0%

commit v1 on v0

--- a/solution.py
+++ b/solution.py
@@ -7,6 +7,12 @@
 NT = 16384
 NF = 1024
 TOUT = 1024
+
+
+def swap_blocks(x, axis, split, join):
+    cells = jnp.split(x, lax.axis_size(axis), axis=split)
+    received = lax.all_to_all(jnp.stack(cells), axis, 0, 0)
+    return jnp.concatenate(received, axis=join)
 
 
 def shifted(block, axis, distance):
@@ -154,7 +160,7 @@
     )
     return jnp.einsum(
         "kcfm,cft->kmt",
-        lax.all_to_all(state_all, "fq", split_axis=0, concat_axis=2, tiled=True),
+        swap_blocks(state_all, "fq", 0, 2),
         inverse,
         preferred_element_type=jnp.float32,
     ).astype(jnp.bfloat16)

time: 2040 us -> 2040 us (level)
    all_to_all x2 -> x0, local copies, waits for them, and re-layouts: 79.4 us -> none  [on_device(): lax.all_to_all(state_all, 'fq', split_axis=0, concat_axis=2, tiled=True)]
    reshape x0 -> x2, local copies, waits for them, and re-layouts: none -> 79.4 us  [swap_blocks(): return jnp.concatenate(received, axis=join)]
    while x262, local copies, waits for them, and re-layouts: 73.4 us -> 43.8 us
    another operation x3 -> x4, local copies, waits for them, and re-layouts: 48.8 us -> 61.3 us
where the time goes in v1:
time: 2040 us; the launch traced here: 2020 us
  other arithmetic  938 us (46%)
  waiting for transfers between devices  632 us (31%)
  local copies, waits for them, and re-layouts  298 us (15%)
  matrix products  89.7 us (4%)
  starting transfers between devices  59.1 us (3%)
    all_to_all x1, waiting for transfers between devices, swap_blocks(): received = lax.all_to_all(jnp.stack(cells), axis, 0, 0)  536 us
    dynamic_update_slice x96, other arithmetic, on_device(): lax.scan(march_down, (zeros, identity), (forcing, damping))  259 us
    while x78, other arithmetic  119 us
    dynamic_slice x128, local copies, waits for them, and re-layouts, on_device(): lax.scan(march_down, (zeros, identity), (forcing, damping))  100 us
    dynamic_update_slice x32, other arithmetic, on_device(): lax.scan(carry_up, from_above, (damping_up, partial_sum, lifted_down), re...  100 us
    ppermute x14, waiting for transfers between devices, shifted(): return lax.ppermute(block, axis, route)  92.6 us
    add x32, other arithmetic, march_upward(): state = cmul(factor, state) + term  89.1 us
    add x32, other arithmetic, march_down(): state = cmul(factor, state) + term  88.1 us
  transfers between devices with their start and end apart: 17, of which 12 were waited for; matrix products, arithmetic and copies ran while one was open for 2% of the time, Pallas kernels for 0%

profile of v1, /device:TPU:4, one launch (start us, length us, event | category | flops | bytes accessed | tf_op | source)
XLA Modules:
  0.0 2021.9 jit_solution(2429818394373796058)
XLA Ops:
  3.8 110.0 %while.98 = (s32[]{:T(128)}, f32[16,2048]{1,0:T(8,128)S(1)}, bf16[16,16384]{1,0:T(8,128)(2,1)}, s32[1024]{0:T(1024)}, f32[128,1024]{1,0:T(8,128)S(1)}, /*index=5...) while((s32[]{:T(128)}, f32[16,2048]{1,0:T(8,128)S(1)}, ...), condition=%wide.region_1.2_spmd.clone.clone.clone, body=%wide.region_0.1_spmd.clone.clone.clone.sunk | while | flops 184737792 | bytes 51876020 | solution.py:76
  7.0 5.8 fusion.92
  12.9 4.7 fusion.93
  20.7 5.8 fusion.92
  26.6 4.7 fusion.93
  34.5 5.8 fusion.92
  40.4 4.7 fusion.93
  48.2 5.8 fusion.92
  54.1 4.7 fusion.93
  62.0 5.8 fusion.92
  67.8 4.7 fusion.93
  75.7 5.8 fusion.92
  81.6 4.7 fusion.93
  89.4 5.8 fusion.92
  95.3 4.7 fusion.93
  103.2 5.8 fusion.92
  109.1 4.7 fusion.93
  114.4 4.9 all-to-all-start
  120.1 4.0 multiply_sine_fusion
  124.9 4.8 all-to-all-start.1
  131.7 3.7 all-to-all-done.1
  135.5 20.1 fusion.44
  155.6 16.3 broadcast.585.clone
  173.3 315.8 %while.95 = (s32[]{:T(128)}, f32[2,256,768]{2,1,0:T(8,128)}, f32[2,256,768]{2,1,0:T(8,128)}, f32[32,2,256,768]{3,2,1,0:T(8,128)}, f32[32,768]{1,0:T(8,128)}, /*i...) while((s32[]{:T(128)}, f32[2,256,768]{2,1,0:T(8,128)}, ...), condition=%wide.region_3.4_spmd.clone, body=%wide.region_2.3_spmd.clone.sunk | while | flops 5111811 | bytes 33040012 | solution.py:112
  489.1 16.2 broadcast.585.clone.1
  506.7 333.6 %while.96 = (s32[]{:T(128)}, f32[2,256,768]{2,1,0:T(8,128)}, f32[2,256,768]{2,1,0:T(8,128)}, f32[32,2,256,768]{3,2,1,0:T(8,128)}, f32[32,768]{1,0:T(8,128)}, /*i...) while((s32[]{:T(128)}, f32[2,256,768]{2,1,0:T(8,128)}, ...), condition=%wide.region_5.6_spmd.clone, body=%wide.region_4.5_spmd.clone.sunk | while | flops 5505028 | bytes 34612392 | solution.py:123
  530.1 3.4 fusion.87
  540.5 3.4 fusion.87
  561.4 3.4 fusion.87
  592.8 3.4 fusion.87
  634.5 3.4 fusion.87
  645.0 3.4 fusion.87
  665.8 3.4 fusion.87
  676.3 3.4 fusion.87
  749.3 3.4 fusion.87
  770.2 3.4 fusion.87
  780.7 3.4 fusion.87
  791.1 3.4 fusion.87
  801.6 3.4 fusion.87
  840.3 215.6 %while.97 = (s32[]{:T(128)}, f32[2,256,768]{2,1,0:T(8,128)}, f32[2,256,768]{2,1,0:T(8,128)}, f32[2,256,768]{2,1,0:T(8,128)}, f32[2,256,768]{2,1,0:T(8,128)}, /*i...) while((s32[]{:T(128)}, f32[2,256,768]{2,1,0:T(8,128)}, ...), condition=%wide.region_7.8_spmd.clone, body=%wide.region_6.7_spmd.clone.sunk | while | flops 6291459 | bytes 66060612 | solution.py:137
  850.5 10.8 collective-permute-done.1
  863.8 3.4 collective-permute-done
  881.0 11.7 collective-permute-done.1
  904.5 3.7 collective-permute-start.1
  911.2 12.5 collective-permute-done.1
  934.6 4.7 collective-permute-start.1
  942.3 12.8 collective-permute-done.1
  965.9 4.7 collective-permute-start.1
  973.7 13.1 collective-permute-done.1
  997.6 4.7 collective-permute-start.1
  1005.4 13.4 collective-permute-done.1
  1029.6 4.7 collective-permute-start.1
  1037.4 13.8 collective-permute-done.1
  1055.9 16.3 broadcast.585
  1072.2 114.1 %while.93 = (s32[]{:T(128)}, f32[2,256,768]{2,1,0:T(8,128)}, f32[32,2,256,768]{3,2,1,0:T(8,128)}, f32[32,768]{1,0:T(8,128)}, f32[2,256,768]{2,1,0:T(8,128)S(1)}, /*index=5*/s32[]{:T(128)}) while((s32[]{:T(128)}, f32[2,256,768]{2,1,0:T(8,128)}, f32[32,2,256,768]{3,2,1,0:T(8,128)}, f32[32,768]{1,0:T(8,128)}, f32[2,256,768]{2,1,0:T(8,128)S(1)}, ...), condition=%wide.region_9.10_spmd, body=%wide.region_8.9_spmd.sunk | while | flops 1966082 | bytes 18884196 | solution.py:143
  1186.4 8.6 broadcast_in_dim.20
  1195.0 138.6 %while.94 = (s32[]{:T(128)}, f32[2,256,768]{2,1,0:T(8,128)S(1)}, bf16[32,2,256,768]{3,2,1,0:T(8,128)(2,1)}, f32[32,768]{1,0:T(8,128)}, f32[2,256,768]{2,1,0:T(8,...) while((s32[]{:T(128)}, f32[2,256,768]{2,1,0:T(8,128)S(1)}, ...), condition=%wide.region_11.12_spmd, body=%wide.region_10.11_spmd.sunk | while | flops 3538947 | bytes 16524401 | solution.py:150
  1333.6 12.4 slice_bitcast_fusion.3
  1345.9 13.6 pad_maximum_fusion.4
  1359.6 8.8 all-to-all-start.2
  1375.0 535.5 %all-to-all-done.2 = bf16[4,8,2,256,768]{4,3,2,1,0:T(8,128)(2,1)} async-done(((bf16[4,8,2,256,768]{4,3,2,1,0:T(8,128)(2,1)}), bf16[4,8,2,256,768]{4,3,2,1,0:T(8,128)(2,1)}, u32[]{:S(2)}, u32[]{:S(2)}) %all-to-all-start.2) | async-done | bytes 25165856 | tf_op jit(solution)/shard_map/all_to_all | solution.py:14
  1910.5 38.9 %copy.26 = bf16[8,2,4,256,768]{3,2,4,1,0:T(4,128)(2,1)} copy(bf16[8,2,4,256,768]{4,3,1,0,2:T(8,128)(2,1)} %bitcast.14) | data formatting | bytes 50331648 | tf_op jit(solution)/shard_map/reshape | solution.py:15
  1949.4 40.5 %reshape.468 = bf16[8,2,1024,768]{2,3,1,0:T(8,128)(2,1)} reshape(bf16[8,2,4,256,768]{3,2,4,1,0:T(4,128)(2,1)} %copy.26) | data formatting | bytes 50331648 | tf_op jit(solution)/shard_map/reshape | solution.py:15
  1989.9 32.0 %bitcast_convert_fusion = bf16[8,768,1024]{2,1,0:T(8,128)(2,1)} fusion(bf16[8,2,1024,768]{2,3,1,0:T(8,128)(2,1)} %reshape.468, bf16[1,1024,1024]{2,1,0:T(8,128)(2,1)} %get-tuple-element.879, bf16[1,1024,1024]{2,1,0:T(8,128)(2,1)S(1)} %get-tuple-element.878), kind=kOutput, calls=%fused_computation.81 | convolution fusion | flops 25778192384 | bytes 41943040 | tf_op jit(solution)/shard_map/kcfm,cft->kmt/dot_general | solution.py:161
  (1060 shorter events, 998.6 us)
Async XLA Ops:
  0.0 135.4 %copy-start = (bf16[64,768]{1,0:T(8,128)(2,1)S(1)}, bf16[64,768]{1,0:T(8,128)(2,1)}, u32[]{:S(2)}) copy-start(bf16[64,768]{1,0:T(8,128)(2,1)} %param.22) | copy-start | bytes 294916
  3.8 116.3 %copy-start.16 = (f32[768]{0:T(1024)S(1)}, f32[768]{0:T(1024)}, u32[]{:S(2)}) copy-start(f32[768]{0:T(1024)} %param.25) | copy-start | bytes 9220
  113.8 16.0 copy-start.11
  113.8 16.0 copy-start.13
  113.8 10.3 copy-start.18
  114.4 10.5 all-to-all-start
  124.9 10.5 all-to-all-start.1
  155.6 16.3 copy-start.17
  193.3 1.9 copy-start.4
  203.2 1.9 copy-start.4
  213.1 1.9 copy-start.4
  222.9 1.9 copy-start.4
  232.8 1.9 copy-start.4
  242.6 1.9 copy-start.4
  252.5 1.9 copy-start.4
  262.4 1.9 copy-start.4
  272.3 1.9 copy-start.4
  282.1 1.9 copy-start.4
  292.0 1.9 copy-start.4
  301.9 1.9 copy-start.4
  311.8 1.9 copy-start.4
  321.6 1.9 copy-start.4
  331.5 1.9 copy-start.4
  341.4 1.9 copy-start.4
  351.3 1.9 copy-start.4
  361.3 1.9 copy-start.4
  371.1 1.9 copy-start.4
  381.0 1.9 copy-start.4
  390.9 1.9 copy-start.4
  400.8 1.9 copy-start.4
  410.6 1.9 copy-start.4
  840.4 2.3 copy-start.5
  843.1 4.0 copy-start.10
  845.1 16.2 collective-permute-start.1
  848.1 19.0 collective-permute-start
  871.2 1.9 copy-start.5
  873.5 4.0 copy-start.10
  875.5 17.1 collective-permute-start.1
  878.6 17.5 collective-permute-start
  900.1 1.9 copy-start.5
  902.5 5.8 copy-start.10
  904.5 19.2 collective-permute-start.1
  909.3 16.9 collective-permute-start
  930.2 1.9 copy-start.5
  932.5 6.8 copy-start.10
  934.6 20.5 %collective-permute-start.1 = (bf16[2,256,768]{2,1,0:T(8,128)(2,1)}, bf16[2,256,768]{2,1,0:T(8,128)(2,1)}, u32[]{:S(2)}, u32[]{:S(2)}) collective-permute-start(bf16[2,256,768]{2,1,0:T(8,128)(2,1)} %fusion.89), channel_id=1, source_target_pairs={{4,0},{8,4},{12,8},{16,12},{20,16},{24,20},{28,24},{5,1},{9,5},{13... | collective-permute-start | bytes 2359304 | tf_op jit(solution)/shard_map/while/body/eval_jaxpr/ppermute | solution.py:21
  940.4 17.2 collective-permute-start
  961.6 1.9 copy-start.5
  963.9 6.8 copy-start.10
  965.9 20.9 %collective-permute-start.1 = (bf16[2,256,768]{2,1,0:T(8,128)(2,1)}, bf16[2,256,768]{2,1,0:T(8,128)(2,1)}, u32[]{:S(2)}, u32[]{:S(2)}) collective-permute-start(bf16[2,256,768]{2,1,0:T(8,128)(2,1)} %fusion.89), channel_id=1, source_target_pairs={{4,0},{8,4},{12,8},{16,12},{20,16},{24,20},{28,24},{5,1},{9,5},{13... | collective-permute-start | bytes 2359304 | tf_op jit(solution)/shard_map/while/body/eval_jaxpr/ppermute | solution.py:21
  971.8 17.5 collective-permute-start
  993.3 1.9 copy-start.5
  995.6 6.8 copy-start.10
  997.6 21.2 %collective-permute-start.1 = (bf16[2,256,768]{2,1,0:T(8,128)(2,1)}, bf16[2,256,768]{2,1,0:T(8,128)(2,1)}, u32[]{:S(2)}, u32[]{:S(2)}) collective-permute-start(bf16[2,256,768]{2,1,0:T(8,128)(2,1)} %fusion.89), channel_id=1, source_target_pairs={{4,0},{8,4},{12,8},{16,12},{20,16},{24,20},{28,24},{5,1},{9,5},{13... | collective-permute-start | bytes 2359304 | tf_op jit(solution)/shard_map/while/body/eval_jaxpr/ppermute | solution.py:21
  1003.4 17.8 collective-permute-start
  1025.3 1.9 copy-start.5
  1027.6 6.8 copy-start.10
  1029.6 21.5 %collective-permute-start.1 = (bf16[2,256,768]{2,1,0:T(8,128)(2,1)}, bf16[2,256,768]{2,1,0:T(8,128)(2,1)}, u32[]{:S(2)}, u32[]{:S(2)}) collective-permute-start(bf16[2,256,768]{2,1,0:T(8,128)(2,1)} %fusion.89), channel_id=1, source_target_pairs={{4,0},{8,4},{12,8},{16,12},{20,16},{24,20},{28,24},{5,1},{9,5},{13... | collective-permute-start | bytes 2359304 | tf_op jit(solution)/shard_map/while/body/eval_jaxpr/ppermute | solution.py:21
  1035.4 18.1 collective-permute-start
  1186.4 8.6 copy-start.8
  1359.5 8.8 copy-start.14
  1359.6 9.0 copy-start.12
  1359.6 551.0 %all-to-all-start.2 = ((bf16[4,8,2,256,768]{4,3,2,1,0:T(8,128)(2,1)}), bf16[4,8,2,256,768]{4,3,2,1,0:T(8,128)(2,1)}, u32[]{:S(2)}, u32[]{:S(2)}) async-start(bf16[4,8,2,256,768]{4,3,2,1,0:T(8,128)(2,1)} %pad_maximum_fusion.4), calls=%async_computation.2 | async-start | bytes 50331648 | tf_op jit(solution)/shard_map/all_to_all | solution.py:14
  1989.9 32.0 %copy-start.1 = (bf16[64,768]{1,0:T(8,128)(2,1)S(1)}, bf16[64,768]{1,0:T(8,128)(2,1)}, u32[]{:S(2)}) copy-start(bf16[64,768]{1,0:T(8,128)(2,1)} %param.22) | copy-start | bytes 294916
  (95 other events, 155.6 us)
